TPU v7x, 256 devices: a whole 4x4x8 slice. The times are simulated.
256 devices in a mesh: kx: 8 (over z), ht: 8 (over y, core), real: 4 (over x).
Axes of the slice: x: 4, y: 4, z: 8, core: 2. Of those that a mesh axis runs over, the one named last changes fastest.
Arguments:
- velocity: float32 [3, 4, 32, 512, 128], P(None, 'real', 'kx', 'ht'), may hold values from -6 to 6
- low_index: int32 [8], replicated, may hold values from 0 to 31, as said below
- neighbours: int32 [32, 8], P('kx'), may hold values from 0 to 31, as said below
- owner_map: int32 [64], replicated, may hold values from 0 to 63, each once
- mode_counts: int32 [32], P('kx'), may hold values from 16 to 64
- helmholtz: float32 [64, 512, 512], P(('kx', 'ht')), may hold values from -0.25 to 0.25
Outputs:
- velocity_next: float32 [3, 4, 32, 512, 128], P(None, 'real', 'kx', 'ht')
Inputs may be any that keep to these rules, and one draw needn't show every extreme that they name: `low_index`: distinct values. neighbours[m, j] lies within 4 modes of m, counting circularly over the 32 modes; offsets of + 4 and - 4 both occur.
All inputs are finite; a program needn't handle non-finite values.
Results may differ from a plain program's by a relative error of at most 0.0001.
Values sent between devices are 32-bit elements; how exact they have to be, the bound alone decides.
A program may use at most 64 MiB of HBM per device.

v0:
```python
import jax
import jax.numpy as jnp
from jax import lax
from jax.sharding import PartitionSpec as P

dt_step = 0.1


def extended_2(block, sides, width):
    for axis, dim in sides:
        count = lax.axis_size(axis)
        forward = [(i, i + 1) for i in range(count - 1)]
        forward.append((count - 1, 0))
        backward = [(target, source) for source, target in forward]
        low = lax.ppermute(
            lax.slice_in_dim(block, block.shape[dim] - width, None, axis=dim), axis, forward
        )
        high = lax.ppermute(lax.slice_in_dim(block, 0, width, axis=dim), axis, backward)
        block = jnp.concatenate([low, block, high], axis=dim)
    return block


def spanwise_tables(mode_count, point_count):
    column_ids = jnp.arange(2 * mode_count)
    wavenumber = (column_ids // 2).astype(jnp.float32)
    imag_part = column_ids % 2
    positions = 2.0 * jnp.pi * jnp.arange(point_count).astype(jnp.float32) / point_count
    phases = wavenumber[:, None] * positions[None, :]
    forward = jnp.where(imag_part[:, None] == 0, jnp.cos(phases), -jnp.sin(phases)) / jnp.sqrt(
        jnp.float32(mode_count)
    )
    backward = forward.T * (2.0 * mode_count / point_count)
    return (forward, backward)


def apply_inverse(block, helmholtz, kx_count, ht_count, slots_dev, rows_ht):
    components, reals_dev, band_modes = (block.shape[0], block.shape[1], block.shape[2])
    regrouped = block.reshape(
        components, reals_dev, band_modes, kx_count, ht_count, slots_dev, 2, rows_ht
    )
    regrouped = regrouped.transpose(0, 1, 3, 2, 5, 6, 4, 7)
    regrouped = regrouped.reshape(
        components, reals_dev, kx_count * band_modes, slots_dev, 2, ht_count * rows_ht
    )
    solved = jnp.einsum("syx,crmspx->crmspy", helmholtz, regrouped, precision=lax.Precision.HIGHEST)
    solved = solved.reshape(
        components, reals_dev, kx_count, band_modes, slots_dev, 2, ht_count, rows_ht
    )
    solved = solved.transpose(0, 1, 3, 2, 6, 4, 5, 7)
    return solved.reshape(block.shape)


def local(velocity, low_index, neighbours, owner_map, mode_counts, helmholtz):
    highest = lax.Precision.HIGHEST
    components, reals_dev, band_modes, rows_ht, columns = velocity.shape
    kz_modes = columns // 2
    forward, backward = spanwise_tables(kz_modes, 4 * kz_modes)
    kx_count = lax.axis_size("kx")
    ht_count = lax.axis_size("ht")
    kx_total = band_modes * kx_count
    realizations = reals_dev * lax.axis_size("real")
    owners = kx_count * ht_count
    slots_dev = kz_modes // owners
    width_out = slots_dev * 2 * rows_ht
    low_members = low_index.shape[0]
    band_start = lax.axis_index("kx") * band_modes
    global_modes = band_start + jnp.arange(band_modes, dtype=jnp.int32)
    low_select = (low_index[:, None] == global_modes[None, :]).astype(jnp.float32)
    high_mask = 1.0 - jnp.sum(low_select, axis=0)
    offsets = (neighbours - global_modes[:, None] + kx_total // 2) % kx_total - kx_total // 2
    local_partner = jnp.arange(band_modes, dtype=jnp.int32)[:, None] + band_modes + offsets
    column_mask = ((jnp.arange(columns) // 2)[None, :] < mode_counts[:, None]).astype(jnp.float32)
    inverse_map = (
        jnp.zeros((kz_modes,), jnp.int32).at[owner_map].set(jnp.arange(kz_modes, dtype=jnp.int32))
    )
    current = velocity
    physical = jnp.dot(current, forward, precision=highest)
    extended = extended_2(physical, (("kx", 2),), band_modes)
    own_low = jnp.einsum("jm,crmyz->crjyz", low_select, physical, precision=highest)
    low_fields = lax.psum(own_low, "kx")
    high_low = jnp.zeros_like(physical)
    stresses = []
    for member in range(low_members):
        partner = jnp.take(extended, local_partner[:, member], axis=2)
        low_one = low_fields[:, :, member : member + 1]
        high_low = high_low + low_one * partner[1:2] + partner * low_one[1:2]
        weighted = physical * (partner[1:2] * high_mask[None, None, :, None, None])
        stresses.append(jnp.sum(weighted, axis=(1, 2)))
    stress = jnp.stack(stresses, axis=1)
    nonlinear = jnp.dot(high_low, backward, precision=highest)
    summed = lax.psum(stress, ("kx", "real"))
    low_forcing = jnp.dot(summed / realizations, backward, precision=highest)
    forcing = nonlinear * high_mask[None, None, :, None, None]
    forcing = (
        forcing + jnp.einsum("jm,cjyk->cmyk", low_select, low_forcing, precision=highest)[:, None]
    )
    forcing = forcing * column_mask[None, None, :, None, :]
    updated = current + dt_step * forcing
    slotted = jnp.take(
        updated.reshape(components, reals_dev, band_modes, rows_ht, kz_modes, 2), owner_map, axis=4
    )
    outgoing = slotted.reshape(components, reals_dev, band_modes, rows_ht, owners, slots_dev, 2)
    outgoing = outgoing.transpose(0, 1, 2, 4, 5, 6, 3)
    flat_out = outgoing.reshape(components, reals_dev, band_modes, owners, width_out)
    applied = apply_inverse(
        lax.all_to_all(flat_out, ("kx", "ht"), split_axis=3, concat_axis=3, tiled=True),
        helmholtz,
        kx_count,
        ht_count,
        slots_dev,
        rows_ht,
    )
    returned = lax.all_to_all(applied, ("kx", "ht"), split_axis=3, concat_axis=3, tiled=True)
    restored = returned.reshape(components, reals_dev, band_modes, owners, slots_dev, 2, rows_ht)
    restored = restored.transpose(0, 1, 2, 6, 3, 4, 5).reshape(
        components, reals_dev, band_modes, rows_ht, kz_modes, 2
    )
    current = jnp.take(restored, inverse_map, axis=4).reshape(
        components, reals_dev, band_modes, rows_ht, columns
    )
    return current


def solution(mesh):
    in_specs = (
        P(None, "real", "kx", "ht", None),
        P(),
        P("kx", None),
        P(),
        P("kx"),
        P(("kx", "ht"), None, None),
    )
    out_specs = P(None, "real", "kx", "ht", None)
    return jax.shard_map(local, mesh=mesh, in_specs=in_specs, out_specs=out_specs, check_vma=False)
```

profile of v0, /device:TPU:1, one launch (start us, length us, event | category | flops | bytes accessed | tf_op | source)
XLA Modules:
  0.0 327.1 jit_solution(15920989410416831472)
XLA Ops:
  6.6 2.4 fusion.12
  9.0 2.5 collective-permute-start
  11.5 4.0 %collective-permute-start.1 = (f32[3,1,4,64,256]{4,3,2,0,1:T(8,128)S(1)}, f32[3,1,4,64,256]{4,3,2,0,1:T(8,128)}, u32[]{:S(2)}, u32[]{:S(2)}) collective-permute-start(f32[3,1,4,64,256]{4,3,2,0,1:T(8,128)S(1)} %bitcast.259), channel_id=1, source_target_pairs={{32,0},{64,32},{96,64},{128,96},{160,128},{192,160},{224,192},{0,2... | collective-permute-start | bytes 2359304 | tf_op jit(solution)/shard_map/ppermute | solution.py:18
  15.6 3.1 convolution_bitcast_fusion
  19.8 12.9 %collective-permute-done = f32[3,1,4,64,256]{4,3,2,0,1:T(8,128)S(1)} collective-permute-done((f32[3,1,4,64,256]{4,3,2,0,1:T(8,128)S(1)}, f32[3,1,4,64,256]{4,3,2,0,1:T(8,128)S(1)}, u32[]{:S(2)}, u32[]{:S(2)}) %collective-permute-start) | collective-permute-done | bytes 786464 | tf_op jit(solution)/shard_map/ppermute | solution.py:15
  32.7 0.9 copy-done.16
  33.6 1.8 maximum_bitcast_fusion
  35.4 1.6 gather_fusion.7
  37.0 1.5 gather_fusion.5
  38.5 1.5 gather_fusion.4
  40.0 1.5 gather_fusion.3
  41.5 1.5 gather_fusion.2
  43.0 1.5 gather_fusion.1
  44.5 1.5 gather_fusion
  46.0 1.5 gather_fusion.6
  47.5 1.4 bitcast_select_fusion.2
  48.9 1.3 bitcast_select_fusion.4
  50.8 0.6 copy-done.10
  52.1 1.4 multiply_bitcast_fusion.1
  55.4 3.9 %stack.35 = f32[3,8,64,256]{3,1,2,0:T(8,128)} concatenate(f32[3,1,64,256]{3,1,2,0:T(1,128)S(1)} %stack.27, f32[3,1,64,256]{3,1,2,0:T(1,128)S(1)} %stack.28, f32[3,1,64,256]{3,1,2,0:T(1,128)S(1)} %stack.29, f32[3,1,64,256]{3,1,2,0:T(1,128)S(1)} %stack.30, f32[3,1,64,256]{3,1,2,0:T(1,128)S(1)} %stack.31, f32[3,1,64,256]{3,1,2,0:T(1,128)S(1)} %stack.32, ...), dimensions={1} | concatenate | bytes 3145728 | tf_op jit(solution)/shard_map/stack | solution.py:89
  60.4 35.1 %all-reduce.3.cloned.1.call-done = f32[3,1,8,64,256]{4,2,3,0,1:T(8,128)} async-done(((f32[3,1,8,64,256]{4,2,3,0,1:T(8,128)}), f32[3,1,8,64,256]{4,2,3,0,1:T(8,128)}) %all-reduce.3.cloned.1.call-update) | async-done | bytes 1572880 | tf_op jit(solution)/shard_map/psum | solution.py:80
  95.5 7.7 %fusion.51 = (f32[3,1,1,64,256]{4,2,3,0,1:T(1,128)S(1)}, f32[3,1,1,64,256]{4,2,3,0,1:T(1,128)S(1)}, f32[3,1,1,64,256]{4,2,3,0,1:T(1,128)S(1)}, f32[3,1,1,64,256]...) fusion(f32[3,1,8,64,256]{4,2,3,0,1:T(8,128)} %all-reduce.3.clon, ...), kind=kLoop, calls=%fused_computation.172 | loop fusion | bytes 3145728 | tf_op jit(solution)/shard_map/slice | solution.py:85
  103.2 0.7 copy.102
  103.8 0.7 copy.103
  104.5 0.7 copy.104
  105.2 0.7 copy.105
  105.9 0.7 copy.106
  106.6 0.7 copy.107
  107.3 0.7 copy.108
  108.0 0.7 copy.109
  108.7 3.5 %fusion.52 = (f32[1,1,1,64,256]{4,2,3,0,1:T(1,128)S(1)}, f32[1,1,1,64,256]{4,2,3,0,1:T(1,128)S(1)}, f32[1,1,1,64,256]{4,2,3,0,1:T(1,128)S(1)}, f32[1,1,1,64,256]...) fusion(f32[3,1,8,64,256]{4,2,3,0,1:T(8,128)} %all-reduce.3.clon, ...), kind=kLoop, calls=%fused_computation.173 | loop fusion | bytes 1048576 | tf_op jit(solution)/shard_map/slice | solution.py:86
  112.2 0.6 copy.112
  113.5 0.6 copy.114
  115.3 0.6 copy.117
  116.0 133.7 %all-reduce.5.cloned.1.call-done = f32[3,8,64,256]{3,1,2,0:T(8,128)} async-done(((f32[3,8,64,256]{3,1,2,0:T(8,128)}), f32[3,8,64,256]{3,1,2,0:T(8,128)}) %all-reduce.5.cloned.1.call-update) | async-done | bytes 1572880 | tf_op jit(solution)/shard_map/psum | solution.py:91
  249.7 3.5 %fusion = f32[3,8,64,128]{3,1,2,0:T(8,128)S(1)} fusion(f32[3,8,64,256]{3,1,2,0:T(8,128)} %all-reduce.5.cloned.1.call-done, f32[256]{0:T(256)S(1)} %convert_multiply_fusion, f32[128]{0:T(128)} %copy-done.17, pred[128]{0:T(512)(128)(4,1)S(1)} %fusion.42), kind=kOutput, calls=%fused_computation.12 | convolution fusion | flops 604504064 | bytes 2360960 | tf_op jit(solution)/shard_map/dot_general | solution.py:92
  253.2 1.2 fusion.50
  254.4 5.9 %fusion.6 = f32[3,1,4,64,128]{4,3,2,0,1:T(8,128)} fusion(f32[3,1,4,64,128]{4,3,2,1,0:T(8,128)S(1)} %copy-done.14, f32[3,64,128,4]{2,3,1,0:T(4,128)S(1)} %fusion.50, f32[4,128]{1,0:T(4,128)S(1)} %compare_convert_fusion.1, f32[4]{0:T(128)} %copy-done.27, f32[256]{0:T(256)S(1)} %convert_multiply_fusion, f32[128]{0:T(128)} %copy-done.17, ...), kind=kOutput, calls=%fused_computation.21 | convolution fusion | flops 310280192 | bytes 11669168 | tf_op jit(solution)/shard_map/dot_general | solution.py:90
  260.3 1.3 copy.38
  262.1 1.0 gather_fusion.8
  264.4 27.5 %all_to_all.10 = f32[3,1,4,64,128]{4,2,0,1,3:T(4,128)S(1)} all-to-all(f32[3,1,4,64,128]{4,2,0,1,3:T(4,128)S(1)} %reshape.457), channel_id=1, replica_groups=mesh['kx'=8,'ht'=8,'real'=4] {'kx','ht'}, dimensions={3} | all-to-all | bytes 786432 | tf_op jit(solution)/shard_map/all_to_all | solution.py:106
  292.8 1.5 convolution_bitcast_fusion.1
  294.9 1.3 reshape.459
  296.2 5.5 %all-to-all-start.1 = ((f32[3,1,4,64,128]{4,2,0,1,3:T(4,128)}), f32[3,1,4,64,128]{4,2,0,1,3:T(4,128)S(1)}, u32[]{:S(2)}, u32[]{:S(2)}) async-start(f32[3,1,4,64,128]{4,2,0,1,3:T(4,128)} %reshape.459), calls=%async_computation.1 | async-start | bytes 786432 | tf_op jit(solution)/shard_map/all_to_all | solution.py:113
  301.6 0.9 scatter_custom_fusion
  302.6 14.2 %all-to-all-done.1 = f32[3,1,4,64,128]{4,2,0,1,3:T(4,128)S(1)} async-done(((f32[3,1,4,64,128]{4,2,0,1,3:T(4,128)}), f32[3,1,4,64,128]{4,2,0,1,3:T(4,128)S(1)}, u32[]{:S(2)}, u32[]{:S(2)}) %all-to-all-start.1) | async-done | bytes 393248 | tf_op jit(solution)/shard_map/all_to_all | solution.py:113
  317.5 1.1 gather_fusion.9
  319.3 1.0 copy.49
  (145 shorter events, 11.2 us)
Async XLA Ops:
  6.5 286.2 %copy-start = (f32[1,512,512]{2,1,0:T(8,128)S(1)}, f32[1,512,512]{2,1,0:T(8,128)}, u32[]{:S(2)}) copy-start(f32[1,512,512]{2,1,0:T(8,128)} %param.15) | copy-start | bytes 3145732
  6.5 89.0 %all-reduce.3.cloned.1.call-start = ((), (), s32[]{:S(2)}) async-start(), calls=%async_computation.2 | async-start | bytes 3145728 | tf_op jit(solution)/shard_map/psum | solution.py:80
  6.6 12.2 %copy-start.17 = (f32[128]{0:T(128)}, f32[128]{0:T(128)S(1)}, u32[]{:S(2)}) copy-start(f32[128]{0:T(128)S(1)} %fusion.45) | copy-start | bytes 1540
  6.6 12.2 %copy-start.28 = (s32[4,8]{1,0:T(4,128)S(1)}, s32[4,8]{1,0:T(4,128)}, u32[]{:S(2)}) copy-start(s32[4,8]{1,0:T(4,128)} %param.12) | copy-start | bytes 388
  6.6 13.0 %copy-start.29 = (s32[8]{0:T(128)S(1)}, s32[8]{0:T(128)}, u32[]{:S(2)}) copy-start(s32[8]{0:T(128)} %param.11) | copy-start | bytes 100
  9.0 23.7 %copy-start.1 = (f32[256,3,4,64]{0,3,2,1:T(8,128)}, f32[256,3,4,64]{0,3,2,1:T(8,128)S(1)}, u32[]{:S(2)}) copy-start(f32[256,3,4,64]{0,3,2,1:T(8,128)S(1)} %fusion.12) | copy-start | bytes 2359300
  9.0 23.7 %collective-permute-start = (f32[3,1,4,64,256]{4,3,2,0,1:T(8,128)S(1)}, f32[3,1,4,64,256]{4,3,2,0,1:T(8,128)S(1)}, u32[]{:S(2)}, u32[]{:S(2)}) collective-permute-start(f32[3,1,4,64,256]{4,3,2,0,1:T(8,128)S(1)} %bitcast.258), channel_id=1, source_target_pairs={{0,32},{32,64},{64,96},{96,128},{128,160},{160,192},{192,224},{224... | collective-permute-start | bytes 2359304 | tf_op jit(solution)/shard_map/ppermute | solution.py:15
  11.5 22.1 %collective-permute-start.1 = (f32[3,1,4,64,256]{4,3,2,0,1:T(8,128)S(1)}, f32[3,1,4,64,256]{4,3,2,0,1:T(8,128)}, u32[]{:S(2)}, u32[]{:S(2)}) collective-permute-start(f32[3,1,4,64,256]{4,3,2,0,1:T(8,128)S(1)} %bitcast.259), channel_id=1, source_target_pairs={{32,0},{64,32},{96,64},{128,96},{160,128},{192,160},{224,192},{0,2... | collective-permute-start | bytes 2359304 | tf_op jit(solution)/shard_map/ppermute | solution.py:18
  15.6 19.9 %copy-start.18 = (s32[4]{0:T(128)}, s32[4]{0:T(128)S(1)}, u32[]{:S(2)}) copy-start(s32[4]{0:T(128)S(1)} %get-tuple-element.70) | copy-start | bytes 52
  18.8 230.9 %all-reduce.5.cloned.1.call-start = ((), (), s32[]{:S(2)}) async-start(), calls=%async_computation.3 | async-start | bytes 3145728 | tf_op jit(solution)/shard_map/psum | solution.py:91
  19.2 28.2 %copy-start.19 = (pred[4]{0:T(512)(128)(4,1)}, pred[4]{0:T(512)(128)(4,1)S(1)}, u32[]{:S(2)}) copy-start(pred[4]{0:T(512)(128)(4,1)S(1)} %compare_and_fusion.2) | copy-start | bytes 16
  19.3 29.6 %copy-start.20 = (pred[4]{0:T(512)(128)(4,1)}, pred[4]{0:T(512)(128)(4,1)S(1)}, u32[]{:S(2)}) copy-start(pred[4]{0:T(512)(128)(4,1)S(1)} %compare_and_fusion.4) | copy-start | bytes 16
  19.3 30.9 %copy-start.21 = (pred[4]{0:T(512)(128)(4,1)}, pred[4]{0:T(512)(128)(4,1)S(1)}, u32[]{:S(2)}) copy-start(pred[4]{0:T(512)(128)(4,1)S(1)} %compare_and_fusion.5) | copy-start | bytes 16
  19.3 31.1 %copy-start.22 = (pred[4]{0:T(512)(128)(4,1)}, pred[4]{0:T(512)(128)(4,1)S(1)}, u32[]{:S(2)}) copy-start(pred[4]{0:T(512)(128)(4,1)S(1)} %compare_and_fusion.6) | copy-start | bytes 16
  19.4 31.2 %copy-start.23 = (pred[4]{0:T(512)(128)(4,1)}, pred[4]{0:T(512)(128)(4,1)S(1)}, u32[]{:S(2)}) copy-start(pred[4]{0:T(512)(128)(4,1)S(1)} %compare_and_fusion.7) | copy-start | bytes 16
  19.4 31.4 %copy-start.24 = (pred[4]{0:T(512)(128)(4,1)}, pred[4]{0:T(512)(128)(4,1)S(1)}, u32[]{:S(2)}) copy-start(pred[4]{0:T(512)(128)(4,1)S(1)} %compare_and_fusion.8) | copy-start | bytes 16
  19.7 31.8 %copy-start.25 = (pred[4]{0:T(512)(128)(4,1)}, pred[4]{0:T(512)(128)(4,1)S(1)}, u32[]{:S(2)}) copy-start(pred[4]{0:T(512)(128)(4,1)S(1)} %compare_and_fusion.9) | copy-start | bytes 16
  19.8 32.1 %copy-start.26 = (pred[4]{0:T(512)(128)(4,1)}, pred[4]{0:T(512)(128)(4,1)S(1)}, u32[]{:S(2)}) copy-start(pred[4]{0:T(512)(128)(4,1)S(1)} %compare_and_fusion.3) | copy-start | bytes 16
  19.8 32.3 %copy-start.27 = (f32[4]{0:T(128)}, f32[4]{0:T(128)S(1)}, u32[]{:S(2)}) copy-start(f32[4]{0:T(128)S(1)} %broadcast_subtract_fusion) | copy-start | bytes 52
  32.7 0.9 copy-start.16
  47.5 2.8 copy-start.5
  47.5 3.0 copy-start.6
  48.9 1.7 copy-start.8
  50.3 1.2 copy-start.10
  50.4 1.2 copy-start.12
  50.6 1.4 copy-start.13
  52.1 1.6 copy-start.2
  55.3 3.9 %copy-start.33 = (s32[64]{0:T(128)S(1)}, s32[64]{0:T(128)}, u32[]{:S(2)}) copy-start(s32[64]{0:T(128)} %param.13) | copy-start | bytes 772
  55.4 5.0 %copy-start.32 = (s32[4]{0:T(128)S(1)}, s32[4]{0:T(128)}, u32[]{:S(2)}) copy-start(s32[4]{0:T(128)} %param.14) | copy-start | bytes 52
  59.3 0.5 copy-start.31
  112.2 142.2 %copy-start.3 = (f32[4,3,64,256]{3,2,1,0:T(8,128)S(1)}, f32[4,3,64,256]{3,2,1,0:T(8,128)}, u32[]{:S(2)}) copy-start(f32[4,3,64,256]{3,2,1,0:T(8,128)} %gather_fusion.7) | copy-start | bytes 2359300
  112.2 142.2 %copy-start.4 = (f32[4,3,64,256]{3,2,1,0:T(8,128)S(1)}, f32[4,3,64,256]{3,2,1,0:T(8,128)}, u32[]{:S(2)}) copy-start(f32[4,3,64,256]{3,2,1,0:T(8,128)} %gather_fusion.5) | copy-start | bytes 2359300
  249.7 4.7 %copy-start.7 = (f32[4,3,64,256]{3,2,1,0:T(8,128)S(1)}, f32[4,3,64,256]{3,2,1,0:T(8,128)}, u32[]{:S(2)}) copy-start(f32[4,3,64,256]{3,2,1,0:T(8,128)} %gather_fusion.3) | copy-start | bytes 2359300
  249.7 4.7 %copy-start.9 = (f32[4,3,64,256]{3,2,1,0:T(8,128)S(1)}, f32[4,3,64,256]{3,2,1,0:T(8,128)}, u32[]{:S(2)}) copy-start(f32[4,3,64,256]{3,2,1,0:T(8,128)} %gather_fusion.2) | copy-start | bytes 2359300
  249.7 4.7 %copy-start.11 = (f32[4,3,64,256]{3,2,1,0:T(8,128)S(1)}, f32[4,3,64,256]{3,2,1,0:T(8,128)}, u32[]{:S(2)}) copy-start(f32[4,3,64,256]{3,2,1,0:T(8,128)} %gather_fusion.1) | copy-start | bytes 2359300
  249.7 4.7 %copy-start.14 = (f32[3,1,4,64,128]{4,3,2,1,0:T(8,128)S(1)}, f32[3,1,4,64,128]{4,3,2,1,0:T(8,128)}, u32[]{:S(2)}) copy-start(f32[3,1,4,64,128]{4,3,2,1,0:T(8,128)} %param.10) | copy-start | bytes 1179652
  249.7 4.7 %copy-start.15 = (f32[4,64,256]{2,1,0:T(8,128)S(1)}, f32[4,64,256]{2,1,0:T(8,128)}, u32[]{:S(2)}) copy-start(f32[4,64,256]{2,1,0:T(8,128)} %get-tuple-element.40) | copy-start | bytes 786436
  262.1 1.1 copy-start.30
  296.2 20.6 %all-to-all-start.1 = ((f32[3,1,4,64,128]{4,2,0,1,3:T(4,128)}), f32[3,1,4,64,128]{4,2,0,1,3:T(4,128)S(1)}, u32[]{:S(2)}, u32[]{:S(2)}) async-start(f32[3,1,4,64,128]{4,2,0,1,3:T(4,128)} %reshape.459), calls=%async_computation.1 | async-start | bytes 786432 | tf_op jit(solution)/shard_map/all_to_all | solution.py:113
Sparse Core Ops, SparseCore 0:
  18.9 76.5 all-reduce.2
  98.9 150.7 all-reduce.4
where the time goes:
time: 328 us; the launch traced here: 327 us
  waiting for transfers between devices  196 us (60%)
  local copies, waits for them, and re-layouts  50.8 us (15%)
  blocking collectives  27.5 us (8%)
  matrix products  17.6 us (5%)
  between operations  14.4 us (4%)
  starting transfers between devices  12.1 us (4%)
  other arithmetic  8.77 us (3%)
    psum x1, waiting for transfers between devices, local(): summed = lax.psum(stress, ('kx', 'real'))  134 us
    psum x1, waiting for transfers between devices, local(): low_fields = lax.psum(own_low, 'kx')  35.1 us
    all_to_all x1, blocking collectives, local(): lax.all_to_all(flat_out, ('kx', 'ht'), split_axis=3, concat_axis=3, tiled...  27.5 us
    all_to_all x1, waiting for transfers between devices, local(): lax.all_to_all(applied, ('kx', 'ht'), split_axis=3, concat_axis=3, tiled=...  14.2 us
    ppermute x1, waiting for transfers between devices, extended_2(): lax.ppermute(lax.slice_in_dim(block, block.shape[dim] - width, None, axis...  12.9 us
    gather x8, local copies, waits for them, and re-layouts, local(): partner = jnp.take(extended, local_partner[:, member], axis=2)  12 us
    unnamed x84, local copies, waits for them, and re-layouts  11.8 us
    slice x1, local copies, waits for them, and re-layouts, local(): low_one = low_fields[:, :, member:member + 1]  7.67 us
  transfers between devices with their start and end apart: 5, of which 4 were waited for; matrix products, arithmetic and copies ran while one was open for 15% of the time, Pallas kernels for 0%

commit v1 on v0

--- a/solution.py
+++ b/solution.py
@@ -77,7 +77,7 @@
     physical = jnp.dot(current, forward, precision=highest)
     extended = extended_2(physical, (("kx", 2),), band_modes)
     own_low = jnp.einsum("jm,crmyz->crjyz", low_select, physical, precision=highest)
-    low_fields = lax.psum(own_low, "kx")
+    low_fields = jnp.sum(lax.all_gather(own_low, "kx"), axis=0)
     high_low = jnp.zeros_like(physical)
     stresses = []
     for member in range(low_members):

time: 328 us -> 391 us (1.19)
  waiting for transfers between devices: 196 us -> 265 us
  local copies, waits for them, and re-layouts: 50.8 us -> 41.9 us
  other arithmetic: 8.77 us -> 15.7 us
  matrix products: 17.6 us -> 11.5 us
    psum x1, waiting for transfers between devices: 134 us -> 236 us  [local(): summed = lax.psum(stress, ('kx', 'real'))]
    psum x1 -> x0, waiting for transfers between devices: 35.1 us -> none  [local(): low_fields = lax.psum(own_low, 'kx')]
    unnamed x84 -> x73, local copies, waits for them, and re-layouts: 11.8 us -> 4.87 us
    another operation x9, local copies, waits for them, and re-layouts: 4.95 us -> 11.7 us  [local(): stress = jnp.stack(stresses, axis=1)]
    slice x1, local copies, waits for them, and re-layouts: 7.67 us -> 1.45 us  [local(): low_one = low_fields[:, :, member:member + 1]]
    reduce_sum x0 -> x1, other arithmetic: none -> 6.1 us  [local(): low_fields = jnp.sum(lax.all_gather(own_low, 'kx'), axis=0)]
  transfers between devices with their start and end apart: 5 -> 5, of which waited for: 4 -> 3; matrix products, arithmetic and copies ran while one was open for 15% -> 2% of each run, Pallas kernels for 0% -> 0%
where the time goes in v1:
time: 391 us; the launch traced here: 390 us
  waiting for transfers between devices  265 us (68%)
  local copies, waits for them, and re-layouts  41.9 us (11%)
  blocking collectives  27.5 us (7%)
  between operations  15.8 us (4%)
  other arithmetic  15.7 us (4%)
  starting transfers between devices  12.2 us (3%)
  matrix products  11.5 us (3%)
    psum x1, waiting for transfers between devices, local(): summed = lax.psum(stress, ('kx', 'real'))  236 us
    all_to_all x1, blocking collectives, local(): lax.all_to_all(flat_out, ('kx', 'ht'), split_axis=3, concat_axis=3, tiled...  27.5 us
    ppermute x1, waiting for transfers between devices, extended_2(): lax.ppermute(lax.slice_in_dim(block, block.shape[dim] - width, None, axis...  14.9 us
    all_to_all x1, waiting for transfers between devices, local(): lax.all_to_all(applied, ('kx', 'ht'), split_axis=3, concat_axis=3, tiled=...  14.3 us
    gather x8, local copies, waits for them, and re-layouts, local(): partner = jnp.take(extended, local_partner[:, member], axis=2)  12 us
    another operation x9, local copies, waits for them, and re-layouts, local(): stress = jnp.stack(stresses, axis=1)  11.7 us
  transfers between devices with their start and end apart: 5, of which 3 were waited for; matrix products, arithmetic and copies ran while one was open for 2% of the time, Pallas kernels for 0%

profile of v1, /device:TPU:1, one launch (start us, length us, event | category | flops | bytes accessed | tf_op | source)
XLA Modules:
  0.0 389.8 jit_solution(3383357565651062778)
XLA Ops:
  7.4 2.4 fusion.12
  9.8 2.5 collective-permute-start
  12.4 4.0 %collective-permute-start.1 = (f32[3,1,4,64,256]{4,3,2,0,1:T(8,128)S(1)}, f32[3,1,4,64,256]{4,3,2,0,1:T(8,128)}, u32[]{:S(2)}, u32[]{:S(2)}) collective-permute-start(f32[3,1,4,64,256]{4,3,2,0,1:T(8,128)S(1)} %bitcast.266), channel_id=1, source_target_pairs={{32,0},{64,32},{96,64},{128,96},{160,128},{192,160},{224,192},{0,2... | collective-permute-start | bytes 2359304 | tf_op jit(solution)/shard_map/ppermute | solution.py:18
  16.4 0.8 fusion.41
  17.7 0.8 fusion.38
  18.6 14.9 %collective-permute-done = f32[3,1,4,64,256]{4,3,2,0,1:T(8,128)S(1)} collective-permute-done((f32[3,1,4,64,256]{4,3,2,0,1:T(8,128)S(1)}, f32[3,1,4,64,256]{4,3,2,0,1:T(8,128)S(1)}, u32[]{:S(2)}, u32[]{:S(2)}) %collective-permute-start) | collective-permute-done | bytes 786464 | tf_op jit(solution)/shard_map/ppermute | solution.py:15
  33.5 0.9 copy-done.24
  34.4 1.8 maximum_bitcast_fusion
  36.2 1.5 gather_fusion.7
  37.8 1.5 gather_fusion.5
  39.3 1.5 gather_fusion.4
  40.7 1.5 gather_fusion.3
  42.2 1.5 gather_fusion.2
  43.7 1.5 gather_fusion.1
  45.2 1.5 gather_fusion
  46.7 1.5 gather_fusion.6
  48.2 1.4 bitcast_select_fusion.2
  49.6 1.3 bitcast_select_fusion.4
  51.5 0.6 copy-done.9
  52.8 1.4 multiply_bitcast_fusion.1
  54.8 0.8 stack.27
  55.7 0.8 stack.28
  56.5 0.8 stack.29
  57.3 0.8 stack.30
  58.1 0.8 stack.31
  58.9 0.8 stack.32
  59.7 0.8 stack.33
  60.5 0.8 stack.34
  61.3 5.2 %stack.35 = f32[3,8,64,256]{3,1,2,0:T(8,128)} concatenate(f32[3,1,64,256]{3,1,2,0:T(1,128)} %stack.27, f32[3,1,64,256]{3,1,2,0:T(1,128)} %stack.28, f32[3,1,64,256]{3,1,2,0:T(1,128)} %stack.29, f32[3,1,64,256]{3,1,2,0:T(1,128)} %stack.30, f32[3,1,64,256]{3,1,2,0:T(1,128)} %stack.31, f32[3,1,64,256]{3,1,2,0:T(1,128)} %stack.32, f32[3,1,64,256]{3,1,2,0:T(1,128)} %stack.33, ...), dimensions={1} | concatenate | bytes 3145728 | tf_op jit(solution)/shard_map/stack | solution.py:89
  66.8 1.3 convolution_bitcast_fusion
  68.2 1.6 copy.35
  70.0 235.8 %all-reduce.2.cloned.1.call-done = f32[3,8,64,256]{3,1,2,0:T(8,128)} async-done(((f32[3,8,64,256]{3,1,2,0:T(8,128)}), f32[3,8,64,256]{3,1,2,0:T(8,128)}) %all-reduce.2.cloned.1.call-update) | async-done | bytes 1572880 | tf_op jit(solution)/shard_map/psum | solution.py:91
  305.8 3.3 fusion
  309.7 6.1 %bitcast_reduce_fusion = f32[3,8,64,256]{3,2,1,0:T(8,128)S(1)} fusion(f32[8,3,8,64,256]{4,3,2,1,0:T(8,128)} %bitcast.264), kind=kLoop, calls=%fused_computation.11 | loop fusion | flops 2752512 | bytes 14155776 | tf_op jit(solution)/shard_map/reduce_sum | solution.py:80
  315.8 0.9 copy.104
  316.8 1.5 fusion.51
  320.8 2.4 fusion.6
  324.0 1.3 gather_fusion.8
  326.0 0.6 reshape.460
  326.5 27.5 %all_to_all.10 = f32[3,1,4,64,128]{4,2,0,1,3:T(4,128)S(1)} all-to-all(f32[3,1,4,64,128]{4,2,0,1,3:T(4,128)S(1)} %reshape.460), channel_id=1, replica_groups=mesh['kx'=8,'ht'=8,'real'=4] {'kx','ht'}, dimensions={3} | all-to-all | bytes 786432 | tf_op jit(solution)/shard_map/all_to_all | solution.py:106
  354.9 1.5 convolution_bitcast_fusion.1
  356.4 0.6 copy.58
  357.0 1.3 reshape.462
  358.3 5.4 %all-to-all-start.1 = ((f32[3,1,4,64,128]{4,2,0,1,3:T(4,128)}), f32[3,1,4,64,128]{4,2,0,1,3:T(4,128)S(1)}, u32[]{:S(2)}, u32[]{:S(2)}) async-start(f32[3,1,4,64,128]{4,2,0,1,3:T(4,128)} %reshape.462), calls=%async_computation.1 | async-start | bytes 786432 | tf_op jit(solution)/shard_map/all_to_all | solution.py:113
  363.8 0.8 scatter_custom_fusion
  364.6 14.3 %all-to-all-done.1 = f32[3,1,4,64,128]{4,2,0,1,3:T(4,128)S(1)} async-done(((f32[3,1,4,64,128]{4,2,0,1,3:T(4,128)}), f32[3,1,4,64,128]{4,2,0,1,3:T(4,128)S(1)}, u32[]{:S(2)}, u32[]{:S(2)}) %all-to-all-start.1) | async-done | bytes 393248 | tf_op jit(solution)/shard_map/all_to_all | solution.py:113
  379.7 1.1 gather_fusion.9
  381.4 1.0 copy.51
  (136 shorter events, 9.0 us)
Async XLA Ops:
  7.4 347.5 %copy-start = (f32[1,512,512]{2,1,0:T(8,128)S(1)}, f32[1,512,512]{2,1,0:T(8,128)}, u32[]{:S(2)}) copy-start(f32[1,512,512]{2,1,0:T(8,128)} %param.15) | copy-start | bytes 3145732
  7.4 298.4 %all-reduce.2.cloned.1.call-start = ((), (), s32[]{:S(2)}) async-start(), calls=%async_computation.2 | async-start | bytes 3145728 | tf_op jit(solution)/shard_map/psum | solution.py:91
  9.8 23.7 %copy-start.1 = (f32[256,3,4,64]{0,3,2,1:T(8,128)}, f32[256,3,4,64]{0,3,2,1:T(8,128)S(1)}, u32[]{:S(2)}) copy-start(f32[256,3,4,64]{0,3,2,1:T(8,128)S(1)} %fusion.12) | copy-start | bytes 2359300
  9.8 23.7 %collective-permute-start = (f32[3,1,4,64,256]{4,3,2,0,1:T(8,128)S(1)}, f32[3,1,4,64,256]{4,3,2,0,1:T(8,128)S(1)}, u32[]{:S(2)}, u32[]{:S(2)}) collective-permute-start(f32[3,1,4,64,256]{4,3,2,0,1:T(8,128)S(1)} %bitcast.265), channel_id=1, source_target_pairs={{0,32},{32,64},{64,96},{96,128},{128,160},{160,192},{192,224},{224... | collective-permute-start | bytes 2359304 | tf_op jit(solution)/shard_map/ppermute | solution.py:15
  12.4 22.1 %collective-permute-start.1 = (f32[3,1,4,64,256]{4,3,2,0,1:T(8,128)S(1)}, f32[3,1,4,64,256]{4,3,2,0,1:T(8,128)}, u32[]{:S(2)}, u32[]{:S(2)}) collective-permute-start(f32[3,1,4,64,256]{4,3,2,0,1:T(8,128)S(1)} %bitcast.266), channel_id=1, source_target_pairs={{32,0},{64,32},{96,64},{128,96},{160,128},{192,160},{224,192},{0,2... | collective-permute-start | bytes 2359304 | tf_op jit(solution)/shard_map/ppermute | solution.py:18
  33.5 0.9 copy-start.24
  48.2 2.8 copy-start.5
  48.2 2.9 copy-start.6
  49.6 1.7 copy-start.7
  51.0 1.1 copy-start.9
  51.1 1.2 copy-start.11
  51.3 1.3 copy-start.13
  52.8 1.6 copy-start.2
  61.3 5.5 %copy-start.25 = (s32[8]{0:T(128)S(1)}, s32[8]{0:T(128)}, u32[]{:S(2)}) copy-start(s32[8]{0:T(128)} %param.11) | copy-start | bytes 100
  66.6 243.1 %all-gather.3.cloned.1.call-start = ((), (), s32[]{:S(2)}) async-start(), calls=%async_computation.3 | async-start | bytes 14155776 | tf_op jit(solution)/shard_map/all_gather | solution.py:80
  68.2 1.7 copy-start.27
  68.2 1.7 copy-start.26
  316.7 2.3 copy-start.16
  316.7 2.3 copy-start.17
  316.7 2.3 copy-start.18
  316.7 2.3 copy-start.19
  316.7 2.3 copy-start.20
  316.8 2.3 copy-start.21
  316.8 2.3 copy-start.22
  316.8 2.3 copy-start.23
  318.2 1.1 copy-start.14
  318.3 1.2 copy-start.15
  318.6 1.2 copy-start.3
  318.6 1.4 copy-start.4
  318.7 1.7 copy-start.8
  318.7 1.9 copy-start.10
  318.7 2.1 copy-start.12
  358.3 20.6 %all-to-all-start.1 = ((f32[3,1,4,64,128]{4,2,0,1,3:T(4,128)}), f32[3,1,4,64,128]{4,2,0,1,3:T(4,128)S(1)}, u32[]{:S(2)}, u32[]{:S(2)}) async-start(f32[3,1,4,64,128]{4,2,0,1,3:T(4,128)} %reshape.462), calls=%async_computation.1 | async-start | bytes 786432 | tf_op jit(solution)/shard_map/all_to_all | solution.py:113
Sparse Core Ops, SparseCore 0:
  66.7 239.0 all-reduce.1
Sparse Core Ops, SparseCore 1:
  69.9 142.2 all-gather.2
